TPU v7x, 32 devices: a whole 2x2x4 slice. The times are simulated.
32 devices in a mesh: groups: 2 (over x), blk: 16 (over z, y, core).
Axes of the slice: x: 2, y: 2, z: 4, core: 2. Of those that a mesh axis runs over, the one named last changes fastest.
Arguments:
- tokens: bfloat16 [8192, 8192], P(('groups', 'blk')), parts along dimension 0, may hold values from -6 to 6
- shrink_panels: bfloat16 [32, 8192, 64], P(None, 'blk'), may hold values from -0.0625 to 0.0625
- expand_panels: bfloat16 [32, 64, 8192], P(None, None, 'blk'), may hold values from -0.75 to 0.75
- adapter_scale: float32 [32], replicated, may hold values from 0.5 to 2
- block_adapter: int32 [128, 1], P('groups'), parts along dimension 0, may hold values from 0 to 31
- shard_counts: int32 [32], P('groups'), parts along dimension 0, may hold values from 1 to 256, as said below
Outputs:
- update: bfloat16 [8192, 8192], P(('groups', 'blk')), parts along dimension 0
There are 2 independent parts, one for each index of `groups`. A program takes and returns all parts, laid end to end along the dimension named above; an argument that names none is the same for every part. Nothing has to cross between parts.
Inputs may be any that keep to these rules, and one draw needn't show every extreme that they name: `shard_counts`: every shard holds at least one live row; in every draw some shard is full.
All inputs are finite; a program needn't handle non-finite values.
Results may differ from a plain program's by a relative error of at most 0.0049.
Values may be sent and summed in bfloat16 or wider, within the bound.
A program may use at most 128 MiB of HBM per device.

v0:
```python
import functools

import jax
import jax.numpy as jnp
from jax import lax
from jax.experimental import pallas as pl
from jax.experimental.pallas import tpu as pltpu
from jax.sharding import PartitionSpec as P

BLOCK = 64
CHUNKS = 2
SLICES = 2
MESH = pl.DeviceIdType.MESH


def kernel(
    n, groups,
    ids, scale, counts, tok_h, s_h, e_h, out_h,
    tok, ps, pe, gs, ge, fs, fe, ss, se, guest, psum, pgot, acc, shr, out_v,
    loc, st_s, st_r, fw_s, fw_r, ax_s, ax_r, fx_s, fx_r, tk_s, tk_r, pt_s, pt_r, osem, *distant,
):
    g, me = lax.axis_index("groups"), lax.axis_index("blk")
    h, w = n // 2, n // 4
    half, pos, q, u = me // h, me % h, me // w, me % w
    adapters, rank, feats = s_h.shape
    blocks = ss.shape[2]
    thick = rank // SLICES
    share = adapters // groups
    size = share // CHUNKS
    near_inner, near_outer = 1 + half, 3 * half
    far = (2 - half, 3 - 3 * half)
    inside = half * (3 - q) + (1 - half) * q
    inner, outer = inside == 1, inside == 0
    sources, own = (s_h, e_h), (ps, pe)
    others = [
        [distant[(2 * j + p) * SLICES:(2 * j + p + 1) * SLICES] for p in range(2)]
        for j in range(2)
    ]
    sends, far_sends, slots = (gs, ge), (fs, fe), (ss, se)

    local = [
        pltpu.make_async_copy(s_h, ps, loc.at[0]),
        pltpu.make_async_copy(e_h, pe, loc.at[1]),
        pltpu.make_async_copy(tok_h, tok, loc.at[2]),
    ]
    for copy in local:
        copy.start()

    barrier = pltpu.get_barrier_semaphore()

    def greet(group, blk):
        pl.semaphore_signal(
            barrier, inc=1, device_id={"groups": group, "blk": blk}, device_id_type=MESH
        )

    for quarter in far:
        greet(g, quarter * w + u)
    for step in range(1, groups):
        greet((g + step) % groups, me)

    @pl.loop(1, h)
    def _(k):
        greet(g, half * h + (pos + k) % h)

    pl.semaphore_wait(barrier, 2 + (groups - 1) + (h - 1))

    def remote(src, dst, send_sem, recv_sem, group, blk):
        return pltpu.make_async_remote_copy(
            src_ref=src, dst_ref=dst, send_sem=send_sem, recv_sem=recv_sem,
            device_id={"groups": group, "blk": blk}, device_id_type=MESH,
        )

    def part(group, c):
        return pl.ds(group * share + c * size, size)

    def ranks(r):
        return pl.ds(r * thick, thick)

    def across(j, p, r, c):
        return remote(
            sources[p].at[part(g, c), ranks(r)], others[j][p][r].at[part(g, c)],
            st_s.at[p, r, c], st_r.at[j, p, r, c], g, far[0] * w + u,
        )

    def forward(j, p, r, c, step):
        rows = others[j][p][r].at[part(g, c)]
        sem = (j, p, r, c, step - 1)
        return remote(rows, rows, fw_s.at[sem], fw_r.at[sem], (g + step) % groups, me)

    def forwarded(j, p, r, c, step):
        rows = others[j][p][r].at[part((g - step + groups) % groups, c)]
        sem = (j, p, r, c, step - 1)
        return remote(rows, rows, fw_s.at[sem], fw_r.at[sem], (g + step) % groups, me)

    def start_across(j, p):
        for r in range(SLICES):
            for c in range(CHUNKS):
                across(j, p, r, c).start()

    def to_peer(p, d):
        return remote(
            sends[p].at[d], slots[p].at[me], ax_s.at[p, d], ax_r.at[p, me], g, half * h + d
        )

    def to_far_peer(j, p, r, d):
        owner = far[j] * w + u
        return remote(
            far_sends[p].at[j, d, r], slots[p].at[owner, r],
            fx_s.at[j, p, r, d], fx_r.at[j, p, r, u], g, half * h + d,
        )

    def from_near(p, owner):
        rows = slots[p].at[owner]
        return remote(rows, rows, ax_s.at[p, 0], ax_r.at[p, owner], g, me)

    def from_far(j, p, r, v):
        rows = slots[p].at[far[j] * w + v, r]
        return remote(rows, rows, fx_s.at[j, p, r, 0], fx_r.at[j, p, r, v], g, me)

    def near_send(p):
        local[p].wait()

        @pl.loop(1, h + 1)
        def _(k):
            d = (pos + k) % h
            for b in range(blocks):
                panel = own[p][ids[(half * h + d) * blocks + b]]
                for r in range(SLICES):
                    sends[p][d, r, b] = panel[r * thick:(r + 1) * thick]

        @pl.loop(1, h)
        def _(k):
            to_peer(p, (pos + k) % h).start()

        slots[p][me] = sends[p][pos]

    def end_at(k):
        return (near_outer - 2 * half) * w + (u + k) % w

    def side_at(k):
        return (q - 2 * half) * w + (u + k) % w

    def far_send(j, p, r):
        panel = others[j][p][r]

        def pick(d):
            for b in range(blocks):
                far_sends[p][j, d, r, b] = panel[ids[(half * h + d) * blocks + b]]

        if p == 1 or j == 1:
            @pl.loop(0, w)
            def _(k):
                pick(end_at(k))

            @pl.loop(0, w)
            def _(k):
                to_far_peer(j, p, r, end_at(k)).start()

        @pl.loop(1, w + 1)
        def _(k):
            pick(side_at(k))

        @pl.loop(1, w)
        def _(k):
            to_far_peer(j, p, r, side_at(k)).start()

        slots[p][far[j] * w + u, r] = far_sends[p][j, side_at(0), r]

    def columns(owner):
        return pl.ds(pl.multiple_of(owner * feats, feats), feats)

    def visit(k):
        v = (u + k) % w
        return remote(
            tok_h.at[:, columns(far[0] * w + v)], guest.at[u],
            tk_s.at[v], tk_r.at[u], g, near_inner * w + v,
        )

    def visited(v):
        return remote(guest.at[v], guest.at[v], tk_s.at[v], tk_r.at[v], g, me)

    def back(v):
        return remote(psum.at[v], pgot.at[u], pt_s.at[v], pt_r.at[u], g, near_outer * w + v)

    def came_back(v):
        return remote(pgot.at[v], pgot.at[v], pt_s.at[v], pt_r.at[v], g, me)

    def down(rows, panel):
        return lax.dot_general(
            rows, panel, (((1,), (1,)), ((), ())), preferred_element_type=jnp.float32
        )

    @pl.when(inner)
    def _():
        for p in range(2):
            start_across(0, p)
        for p in range(2):
            near_send(p)
        for j, p, r in [(j, p, r) for j in range(2) for p in range(2) for r in range(SLICES)]:
            for c in range(CHUNKS):
                across(j, p, r, c).wait_recv()
                for step in range(1, groups):
                    forward(j, p, r, c, step).start()
            for c in range(CHUNKS):
                for step in range(1, groups):
                    forwarded(j, p, r, c, step).wait_recv()
            far_send(j, p, r)
            if (j, p, r) == (0, 0, SLICES - 1):
                @pl.loop(0, w)
                def _(k):
                    v = (u + k) % w
                    visited(v).wait_recv()
                    for b in range(blocks):
                        rows = guest[v, b * BLOCK:(b + 1) * BLOCK, :]
                        for i in range(SLICES):
                            panel = others[0][0][i][ids[(near_outer * w + v) * blocks + b]]
                            at = (b % 2) * rank + i * thick
                            psum[v, b // 2, :, at:at + thick] = down(rows, panel)

                @pl.loop(0, w)
                def _(k):
                    back((u + k) % w).start()

    @pl.when(outer)
    def _():
        @pl.loop(0, w)
        def _(k):
            visit(k).start()

        near_send(0)
        start_across(1, 0)
        start_across(1, 1)
        near_send(1)

    local[2].wait()
    acc[...] = jnp.zeros_like(acc)
    def each(p, quarter, j, k0, use):
        @pl.loop(0, w)
        def _(k):
            v = (u - k + w) % w

            @pl.when(k >= k0)
            def _():
                if j is None:
                    from_near(p, quarter * w + v).wait_recv()
                else:
                    for r in range(SLICES):
                        from_far(j, p, r, v).wait_recv()

            use(quarter * w + v)

    def panel_of(slot, owner, b):
        return jnp.concatenate([slot[owner, r, b] for r in range(SLICES)], axis=0)

    def shrink(owner):
        for b in range(blocks):
            acc[b] += down(tok[b * BLOCK:(b + 1) * BLOCK, columns(owner)], panel_of(ss, owner, b))

    each(0, q, None, 1, shrink)

    @pl.when(inner)
    def _():
        for j in range(2):
            each(0, far[j], j, 1, shrink)
        each(0, near_outer, None, 0, shrink)

    @pl.when(outer)
    def _():
        each(0, near_inner, None, 0, shrink)

        @pl.loop(0, w)
        def _(k):
            v = (u - k + w) % w
            came_back(v).wait_recv()
            for b in range(blocks):
                at = (b % 2) * rank
                acc[b] += pgot[v, b // 2, :, at:at + rank]

        each(0, far[1], 1, 0, shrink)

    shr[...] = acc[...].astype(shr.dtype)
    count = counts[me]
    row = lax.broadcasted_iota(jnp.int32, (BLOCK, feats), 0)

    def put(owner):
        cols = columns(owner)
        return pltpu.make_async_copy(out_v.at[:, cols], out_h.at[:, cols], osem.at[owner])

    def expand(owner):
        for b in range(blocks):
            wide = jnp.dot(shr[b], panel_of(se, owner, b), preferred_element_type=jnp.float32)
            wide = wide * scale[ids[me * blocks + b]]
            live = row < count - b * BLOCK
            out_v[b * BLOCK:(b + 1) * BLOCK, columns(owner)] = jnp.where(
                live, wide, 0.0
            ).astype(out_v.dtype)
        put(owner).start()

    each(1, q, None, 1, expand)

    @pl.when(inner)
    def _():
        for j in range(2):
            each(1, far[j], j, 1, expand)
        each(1, near_outer, None, 0, expand)

    @pl.when(outer)
    def _():
        each(1, near_inner, None, 0, expand)
        for j in range(2):
            each(1, far[j], j, 0, expand)

    for p in range(2):
        for r in range(SLICES):
            for c in range(CHUNKS):
                across(0, p, r, c).wait_send()

        @pl.loop(1, h)
        def _(k):
            to_peer(p, (pos + k) % h).wait_send()

    @pl.when(inner)
    def _():
        for j, p, r in [(j, p, r) for j in range(2) for p in range(2) for r in range(SLICES)]:
            for c in range(CHUNKS):
                for step in range(1, groups):
                    forward(j, p, r, c, step).wait_send()

            @pl.loop(1, w)
            def _(k):
                to_far_peer(j, p, r, side_at(k)).wait_send()

            if p == 1 or j == 1:
                @pl.loop(0, w)
                def _(k):
                    to_far_peer(j, p, r, end_at(k)).wait_send()

        @pl.loop(0, w)
        def _(k):
            back((u + k) % w).wait_send()

    @pl.when(outer)
    def _():
        @pl.loop(0, w)
        def _(k):
            visit(k).wait_send()

    @pl.loop(0, n)
    def _(owner):
        put(owner).wait()


def body(n, groups, tokens, shrink_panels, expand_panels, adapter_scale, block_adapter, shard_counts):
    rows, width = tokens.shape
    adapters, feats, rank = shrink_panels.shape
    blocks = rows // BLOCK
    h, w = n // 2, n // 4
    bf16 = tokens.dtype
    dma = pltpu.SemaphoreType.DMA
    smem = pl.BlockSpec(memory_space=pltpu.SMEM)
    hbm = pl.BlockSpec(memory_space=pl.ANY)
    panel = pltpu.VMEM((adapters, rank, feats), bf16)
    slice_of = pltpu.VMEM((adapters, rank // SLICES, feats), bf16)
    moved = (SLICES, blocks, rank // SLICES, feats)
    near = pltpu.VMEM((h, *moved), bf16)
    distant = pltpu.VMEM((2, h, *moved), bf16)
    slot = pltpu.VMEM((n, *moved), bf16)
    sums = pltpu.VMEM((w, (blocks + 1) // 2, BLOCK, 2 * rank), jnp.float32)
    return pl.pallas_call(
        functools.partial(kernel, n, groups),
        out_shape=jax.ShapeDtypeStruct((rows, width), bf16),
        in_specs=[smem, smem, smem, hbm, hbm, hbm],
        out_specs=hbm,
        scratch_shapes=[
            pltpu.VMEM((rows, width), bf16),
            panel, panel,
            near, near, distant, distant, slot, slot,
            pltpu.VMEM((w, rows, feats), bf16),
            sums, sums,
            pltpu.VMEM((blocks, BLOCK, rank), jnp.float32),
            pltpu.VMEM((blocks, BLOCK, rank), bf16),
            pltpu.VMEM((rows, width), bf16),
            dma((3,)),
            dma((2, SLICES, CHUNKS)), dma((2, 2, SLICES, CHUNKS)),
            dma((2, 2, SLICES, CHUNKS, groups - 1)), dma((2, 2, SLICES, CHUNKS, groups - 1)),
            dma((2, h)), dma((2, n)), dma((2, 2, SLICES, h)), dma((2, 2, SLICES, w)),
            dma((w,)), dma((w,)), dma((w,)), dma((w,)),
            dma((n,)),
            *[slice_of] * (4 * SLICES),
        ],
        compiler_params=pltpu.CompilerParams(
            collective_id=0, has_side_effects=True, vmem_limit_bytes=60 * 1024 * 1024
        ),
    )(
        block_adapter[:, 0], adapter_scale, shard_counts,
        tokens, jnp.swapaxes(shrink_panels, 1, 2), expand_panels,
    )


def solution(mesh):
    return jax.shard_map(
        functools.partial(body, mesh.shape["blk"], mesh.shape["groups"]),
        mesh=mesh,
        in_specs=(
            P(("groups", "blk"), None),
            P(None, "blk", None),
            P(None, None, "blk"),
            P(),
            P("groups", None),
            P("groups"),
        ),
        out_specs=P(("groups", "blk"), None),
        check_vma=False,
    )
```

profile of v0, /device:TPU:0, one launch (start us, length us, event | category | flops | bytes accessed | tf_op | source)
XLA Modules:
  0.0 132.3 jit_solution(18246567106122502625)
XLA Ops:
  0.0 127.6 %shard_map.64 = bf16[256,8192]{1,0:T(8,128)(2,1)} custom-call(s32[64]{0:T(128)} %bitcast.3, f32[32]{0:T(128)} %scale.1, s32[16]{0:T(128)} %counts.1, bf16[256,8192]{1,0:T(8,128)(2,1)} %tok_h.1, bf16[32,64,512]{2,1,0:T(8,128)(2,1)} %bitcast.2, bf16[32,64,512]{2,1,0:T(8,128)(2,1)} %e_h.1), custom_call_target="tpu_custom_call" | custom-call | tf_op jit(solution)/shard_map/pallas_call | solution.py:369
  127.6 4.6 %copy.8 = bf16[256,8192]{1,0:T(8,128)(2,1)} copy(bf16[256,8192]{1,0:T(8,128)(2,1)} %shard_map.64) | data formatting | bytes 8388608
where the time goes:
time: 133 us; the launch traced here: 132 us
  Pallas kernels  128 us (96%)
  local copies, waits for them, and re-layouts  4.64 us (3%)
    pallas_call x1, Pallas kernels, body(): pl.pallas_call(functools.partial(kernel, n, groups), out_shape=jax.ShapeD...  128 us
    unnamed x1, local copies, waits for them, and re-layouts  4.64 us

commit v1 on v0

--- a/solution.py
+++ b/solution.py
@@ -15,9 +15,9 @@
 
 def kernel(
     n, groups,
-    ids, scale, counts, tok_h, s_h, e_h, out_h,
-    tok, ps, pe, gs, ge, fs, fe, ss, se, guest, psum, pgot, acc, shr, out_v,
-    loc, st_s, st_r, fw_s, fw_r, ax_s, ax_r, fx_s, fx_r, tk_s, tk_r, pt_s, pt_r, osem, *distant,
+    ids, scale, counts, tok_h, s_h, e_h, out_v,
+    tok, ps, pe, gs, ge, fs, fe, ss, se, guest, psum, pgot, acc, shr,
+    loc, st_s, st_r, fw_s, fw_r, ax_s, ax_r, fx_s, fx_r, tk_s, tk_r, pt_s, pt_r, *distant,
 ):
     g, me = lax.axis_index("groups"), lax.axis_index("blk")
     h, w = n // 2, n // 4
@@ -282,10 +282,6 @@
     count = counts[me]
     row = lax.broadcasted_iota(jnp.int32, (BLOCK, feats), 0)
 
-    def put(owner):
-        cols = columns(owner)
-        return pltpu.make_async_copy(out_v.at[:, cols], out_h.at[:, cols], osem.at[owner])
-
     def expand(owner):
         for b in range(blocks):
             wide = jnp.dot(shr[b], panel_of(se, owner, b), preferred_element_type=jnp.float32)
@@ -294,7 +290,6 @@
             out_v[b * BLOCK:(b + 1) * BLOCK, columns(owner)] = jnp.where(
                 live, wide, 0.0
             ).astype(out_v.dtype)
-        put(owner).start()
 
     each(1, q, None, 1, expand)
 
@@ -344,10 +339,6 @@
         @pl.loop(0, w)
         def _(k):
             visit(k).wait_send()
-
-    @pl.loop(0, n)
-    def _(owner):
-        put(owner).wait()
 
 
 def body(n, groups, tokens, shrink_panels, expand_panels, adapter_scale, block_adapter, shard_counts):
@@ -368,9 +359,9 @@
     sums = pltpu.VMEM((w, (blocks + 1) // 2, BLOCK, 2 * rank), jnp.float32)
     return pl.pallas_call(
         functools.partial(kernel, n, groups),
-        out_shape=jax.ShapeDtypeStruct((rows, width), bf16),
+        out_shape=pltpu.VMEM((rows, width), bf16),
         in_specs=[smem, smem, smem, hbm, hbm, hbm],
-        out_specs=hbm,
+        out_specs=pl.BlockSpec(memory_space=pltpu.VMEM),
         scratch_shapes=[
             pltpu.VMEM((rows, width), bf16),
             panel, panel,
@@ -379,17 +370,15 @@
             sums, sums,
             pltpu.VMEM((blocks, BLOCK, rank), jnp.float32),
             pltpu.VMEM((blocks, BLOCK, rank), bf16),
-            pltpu.VMEM((rows, width), bf16),
             dma((3,)),
             dma((2, SLICES, CHUNKS)), dma((2, 2, SLICES, CHUNKS)),
             dma((2, 2, SLICES, CHUNKS, groups - 1)), dma((2, 2, SLICES, CHUNKS, groups - 1)),
             dma((2, h)), dma((2, n)), dma((2, 2, SLICES, h)), dma((2, 2, SLICES, w)),
             dma((w,)), dma((w,)), dma((w,)), dma((w,)),
-            dma((n,)),
             *[slice_of] * (4 * SLICES),
         ],
         compiler_params=pltpu.CompilerParams(
-            collective_id=0, has_side_effects=True, vmem_limit_bytes=60 * 1024 * 1024
+            collective_id=0, has_side_effects=True, vmem_limit_bytes=56 * 1024 * 1024
         ),
     )(
         block_adapter[:, 0], adapter_scale, shard_counts,

time: 133 us -> 130 us (0.977)
  local copies, waits for them, and re-layouts: 4.64 us -> 2.02 us
    unnamed x1, local copies, waits for them, and re-layouts: 4.64 us -> 2.02 us
where the time goes in v1:
time: 130 us; the launch traced here: 129 us
  Pallas kernels  127 us (98%)
  local copies, waits for them, and re-layouts  2.02 us (2%)
    pallas_call x1, Pallas kernels, body(): pl.pallas_call(functools.partial(kernel, n, groups), out_shape=pltpu.VMEM...  127 us

profile of v1, /device:TPU:0, one launch (start us, length us, event | category | flops | bytes accessed | tf_op | source)
XLA Modules:
  0.0 129.0 jit_solution(5393876207055430543)
XLA Ops:
  0.0 127.0 %shard_map.64 = bf16[256,8192]{1,0:T(8,128)(2,1)S(1)} custom-call(s32[64]{0:T(128)} %bitcast.3, f32[32]{0:T(128)} %scale.1, s32[16]{0:T(128)} %counts.1, bf16[256,8192]{1,0:T(8,128)(2,1)} %tok_h.1, bf16[32,64,512]{2,1,0:T(8,128)(2,1)} %bitcast.2, bf16[32,64,512]{2,1,0:T(8,128)(2,1)} %e_h.1), custom_call_target="tpu_custom_call" | custom-call | tf_op jit(solution)/shard_map/pallas_call | solution.py:360
  127.0 2.0 %copy.8 = bf16[256,8192]{1,0:T(8,128)(2,1)} copy(bf16[256,8192]{1,0:T(8,128)(2,1)S(1)} %shard_map.64) | data formatting | bytes 8388608

commit v2 on v1

v2 whole, which is shorter than its diff:
```python
import functools

import jax
import jax.numpy as jnp
from jax import lax
from jax.experimental import pallas as pl
from jax.experimental.pallas import tpu as pltpu
from jax.sharding import PartitionSpec as P

BLOCK = 64
UNIT = 16
MESH = pl.DeviceIdType.MESH


def kernel(
    n, groups,
    ids, scale, counts, ids_h, tok_h, s_h, e_h, out_v,
    tok, ps, pe, ns, ne, fs, far_out, rel_out, ss, se, guest, tokrel, psum, pgot, acc, shr, idx_v, idx_s,
    loc, id_s, id_r, id_c, ns_s, ne_s, fs_s, fo_s, ro_s, sl_r,
    rl_s, rl_r, ac_s, ac_r, fw_s, fw_r, xs_s, xs_r,
    ty_s, ty_r, tk_s, tk_r, pt_s, pt_r, *held,
):
    g, me = lax.axis_index("groups"), lax.axis_index("blk")
    h, w = n // 2, n // 4
    half, q, u = me // h, me // w, me % w
    adapters, rank, feats = s_h.shape
    blocks = ss.shape[2]
    units = rank // UNIT
    per = units // groups
    near_inner, near_outer = 1 + half, 3 * half
    far_inner, far_outer = 2 - half, 3 - 3 * half
    inside = half * (3 - q) + (1 - half) * q
    inner, outer = inside == 1, inside == 0
    side = w // 2
    mate = (u + side) % w
    row_of = u // side
    sources, own, slots = (s_h, e_h), (ps, pe), (ss, se)
    far_s = held[:units]
    rest = held[units:]
    far_e, end_s, end_e, rel_s, rel_e = [rest[i * per:(i + 1) * per] for i in range(5)]
    ends, rels = (end_s, end_e), (rel_s, rel_e)

    local = [
        pltpu.make_async_copy(s_h, ps, loc.at[0]),
        pltpu.make_async_copy(e_h, pe, loc.at[1]),
        pltpu.make_async_copy(tok_h, tok, loc.at[2]),
    ]
    for copy in (local[1], local[0], local[2]):
        copy.start()

    barrier = pltpu.get_barrier_semaphore()

    def greet(group, blk):
        pl.semaphore_signal(
            barrier, inc=1, device_id={"groups": group, "blk": blk}, device_id_type=MESH
        )

    @pl.loop(1, groups * h)
    def _(k):
        greet((g + k // h) % groups, half * h + (me + k) % h)

    @pl.when(inner)
    def _():
        greet(g, far_inner * w + u)

    pl.semaphore_wait(barrier, groups * h - 1 + jnp.where(inner, 1, 0))

    def remote(src, dst, send_sem, recv_sem, group, blk):
        return pltpu.make_async_remote_copy(
            src_ref=src, dst_ref=dst, send_sem=send_sem, recv_sem=recv_sem,
            device_id={"groups": group, "blk": blk}, device_id_type=MESH,
        )

    def unit_of(group, s):
        return group * per + s

    def mine(p, s):
        return sources[p].at[:, pl.ds(pl.multiple_of(unit_of(g, s) * UNIT, UNIT), UNIT)]

    def columns(owner, count=1):
        return pl.ds(pl.multiple_of(owner * feats, feats), count * feats)

    def id_of(step, blk, b):
        if step == 0:
            return ids[blk * blocks + b]
        return idx_s[(g + step) % groups, 0, blk * blocks + b]

    def ids_copy(step):
        return remote(
            ids_h, idx_v.at[g], id_s.at[step - 1], id_r.at[g], (g + step) % groups, me
        )

    def ids_got(step):
        rows = idx_v.at[(g - step + groups) % groups]
        return remote(rows, rows, id_s.at[step - 1], id_r.at[(g - step + groups) % groups], g, me)

    def relay(p, s):
        return remote(
            mine(p, s), rels[p][s], rl_s.at[p, s], rl_r.at[p, s], g, near_inner * w + u
        )

    def across(p, s):
        if p == 1:
            return remote(
                mine(1, s), far_e[s], ac_s.at[1, s], ac_r.at[1, s], g, far_inner * w + u
            )
        raise NotImplementedError

    def forward(p, s):
        return remote(
            rels[p][s], ends[p][s], fw_s.at[p, s], fw_r.at[p, s], g, far_inner * w + u
        )

    def near_copy(p, plane, v):
        buf, sem = ((ns, ns_s), (ne, ne_s))[p]
        at = jnp.where(plane == q, 0, w) + v if p else v
        return remote(
            buf.at[at], slots[p].at[me], sem.at[at], sl_r.at[p, me, 0], g, plane * w + v
        )

    def near_fill(p, plane, v, at):
        buf = (ns, ne)[p]
        for b in range(blocks):
            panel = own[p][id_of(0, plane * w + v, b)]
            for un in range(units):
                buf[at, un, b] = panel[un * UNIT:(un + 1) * UNIT]

    def near_own(p):
        @pl.loop(0, w)
        def _(k):
            v = (u + k) % w
            near_fill(p, q, v, v)

        @pl.loop(1, w)
        def _(k):
            near_copy(p, q, (u + k) % w).start()

        slots[p][me] = (ns, ne)[p][u]

    def near_end():
        @pl.loop(0, w)
        def _(k):
            v = (u + k) % w
            near_fill(1, near_outer, v, w + v)

        @pl.loop(0, w)
        def _(k):
            near_copy(1, near_outer, (u + k) % w).start()

    def part_copy(p, owner, un, buf, sem, step, plane, i, v):
        return remote(
            buf.at[step, i * w + v], slots[p].at[owner, un], sem.at[step, i * w + v],
            sl_r.at[p, owner, un], (g + step) % groups, plane * w + v,
        )

    def part_send(p, src, s, quarter, buf, sem, planes):
        owner, un = quarter * w + u, unit_of(g, s)
        for i, plane in enumerate(planes):
            last = i == len(planes) - 1
            for step in range(groups):
                @pl.loop(0, w)
                def _(k, step=step, plane=plane, i=i):
                    v = (u + k) % w
                    for b in range(blocks):
                        buf[step, i * w + v, b] = src[id_of(step, plane * w + v, b)]

                @pl.loop(1 if last and step == 0 else 0, w)
                def _(k, step=step, plane=plane, i=i):
                    part_copy(p, owner, un, buf, sem, step, plane, i, (u + k) % w).start()

        slots[p][owner, un] = buf[0, (len(planes) - 1) * w + u]

    def part_done(p, s, quarter, buf, sem, planes):
        owner, un = quarter * w + u, unit_of(g, s)
        for i, plane in enumerate(planes):
            last = i == len(planes) - 1
            for step in range(groups):
                @pl.loop(1 if last and step == 0 else 0, w)
                def _(k, step=step, plane=plane, i=i):
                    part_copy(p, owner, un, buf, sem, step, plane, i, (u + k) % w).wait_send()

    def part_got(p, owner, un):
        rows = slots[p].at[owner, un]
        return remote(rows, rows, sl_s_dummy(), sl_r.at[p, owner, un], g, me)

    def sl_s_dummy():
        return loc.at[3]

    def full_got(p, owner):
        rows = slots[p].at[owner]
        return remote(rows, rows, sl_s_dummy(), sl_r.at[p, owner, 0], g, me)

    def cross_s(step, s):
        un = unit_of(g, s)
        return [
            (un == i, remote(
                s_h.at[:, pl.ds(i * UNIT, UNIT)], far_s[i], ac_s.at[0, s], ac_r.at[0, i],
                g, far_inner * w + u,
            )) for i in range(units)
        ]

    def start_cross_s(s):
        for chosen, copy in cross_s(0, s):
            @pl.when(chosen)
            def _(copy=copy):
                copy.start()

    def share_s(i, step):
        return remote(
            far_s[i], far_s[i], xs_s.at[i, step - 1], xs_r.at[i], (g + step) % groups, me
        )

    def take_s(s):
        un = unit_of(g, s)
        for i in range(units):
            @pl.when(un == i)
            def _(i=i):
                remote(far_s[i], far_s[i], ac_s.at[0, s], ac_r.at[0, i], g, me).wait_recv()
                for step in range(1, groups):
                    share_s(i, step).start()

    def shared_s():
        for i in range(units):
            @pl.when(i // per != g)
            def _(i=i):
                remote(far_s[i], far_s[i], xs_s.at[i, 0], xs_r.at[i], g, me).wait_recv()

    def far_copy(v):
        return remote(
            fs.at[v], ss.at[far_inner * w + u], fs_s.at[v], sl_r.at[0, far_inner * w + u, 0],
            g, near_inner * w + v,
        )

    def far_own():
        @pl.loop(0, w)
        def _(k):
            v = (u + k) % w
            for b in range(blocks):
                a = id_of(0, near_inner * w + v, b)
                for i in range(units):
                    fs[v, i, b] = far_s[i][a]

        @pl.loop(1, w)
        def _(k):
            far_copy((u + k) % w).start()

        ss[far_inner * w + u] = fs[u]

    def visit_quarter(f):
        return (near_inner, far_inner)[f]

    def pass_rows(f):
        return remote(
            tok_h.at[:, columns(visit_quarter(f) * w + (mate // side) * side, side)],
            tokrel.at[f], ty_s.at[f], ty_r.at[f], g, near_outer * w + mate,
        )

    def visit(f, i):
        v = row_of * side + i
        return remote(
            tok_h.at[:, columns(visit_quarter(f) * w + v)], guest.at[f, u],
            tk_s.at[f, 0, i], tk_r.at[f, u], g, near_inner * w + v,
        )

    def visit_mate(f, i):
        v = row_of * side + i
        return remote(
            tokrel.at[f, :, pl.ds(i * feats, feats)], guest.at[f, mate],
            tk_s.at[f, 1, i], tk_r.at[f, mate], g, near_inner * w + v,
        )

    def visited(f, v):
        return remote(guest.at[f, v], guest.at[f, v], sl_s_dummy(), tk_r.at[f, v], g, me)

    def back(v):
        return remote(psum.at[v], pgot.at[u], pt_s.at[v], pt_r.at[u], g, near_outer * w + v)

    def came_back(v):
        return remote(pgot.at[v], pgot.at[v], sl_s_dummy(), pt_r.at[v], g, me)

    def down(rows, panel):
        return lax.dot_general(
            rows, panel, (((1,), (1,)), ((), ())), preferred_element_type=jnp.float32
        )

    def host(f):
        @pl.loop(0, w)
        def _(k):
            v = (u + k) % w
            visited(f, v).wait_recv()
            for b in range(blocks):
                rows = guest[f, v, b * BLOCK:(b + 1) * BLOCK, :]
                a = id_of(0, near_outer * w + v, b)
                if f == 0:
                    panel = ps[a]
                else:
                    panel = jnp.concatenate([far_s[i][a] for i in range(units)], axis=0)
                at = (b % 2) * rank
                part = down(rows, panel)
                if f == 0:
                    psum[v, b // 2, :, at:at + rank] = part
                else:
                    psum[v, b // 2, :, at:at + rank] += part

    def panel_of(slot, owner, b):
        return jnp.concatenate([slot[owner, i, b] for i in range(units)], axis=0)

    def shrink(owner):
        for b in range(blocks):
            acc[b] += down(tok[b * BLOCK:(b + 1) * BLOCK, columns(owner)], panel_of(ss, owner, b))

    count = counts[me]
    row = lax.broadcasted_iota(jnp.int32, (BLOCK, feats), 0)

    def expand(owner):
        for b in range(blocks):
            wide = jnp.dot(shr[b], panel_of(se, owner, b), preferred_element_type=jnp.float32)
            wide = wide * scale[ids[me * blocks + b]]
            live = row < count - b * BLOCK
            out_v[b * BLOCK:(b + 1) * BLOCK, columns(owner)] = jnp.where(
                live, wide, 0.0
            ).astype(out_v.dtype)

    def each_full(p, quarter, k0, use):
        @pl.loop(0, w)
        def _(k):
            v = (u - k + w) % w

            @pl.when(k >= k0)
            def _():
                full_got(p, quarter * w + v).wait_recv()

            use(quarter * w + v)

    def each_part(p, quarter, k0, use):
        @pl.loop(0, w)
        def _(k):
            v = (u - k + w) % w
            for step in range(groups):
                for s in range(per):
                    un = unit_of((g + step) % groups, s)
                    if step == 0:
                        @pl.when(k >= k0)
                        def _(un=un):
                            part_got(p, quarter * w + v, un).wait_recv()
                    else:
                        part_got(p, quarter * w + v, un).wait_recv()
            use(quarter * w + v)

    both, near = (near_outer, near_inner), (near_inner,)

    def take_end(p, s):
        forward_got = remote(ends[p][s], ends[p][s], fw_s.at[p, s], fw_r.at[p, s], g, me)
        forward_got.wait_recv()
        part_send(p, ends[p][s], s, far_outer, far_out.at[1 + p, s], fo_s.at[1 + p, s], both)

    def take_far_e(s):
        remote(far_e[s], far_e[s], ac_s.at[1, s], ac_r.at[1, s], g, me).wait_recv()
        part_send(1, far_e[s], s, far_inner, far_out.at[0, s], fo_s.at[0, s], both)

    def take_relay(p, s):
        remote(rels[p][s], rels[p][s], rl_s.at[p, s], rl_r.at[p, s], g, me).wait_recv()
        forward(p, s).start()
        part_send(p, rels[p][s], s, near_outer, rel_out.at[p, s], ro_s.at[p, s], near)

    @pl.when(inner)
    def _():
        for step in range(1, groups):
            ids_copy(step).start()
        for s in range(per):
            across(1, s).start()
        local[1].wait()
        near_end()
        near_own(1)
        local[0].wait()
        near_own(0)
        for step in range(1, groups):
            other = (g - step + groups) % groups
            ids_got(step).wait_recv()
            copy = pltpu.make_async_copy(idx_v.at[other], idx_s.at[other], id_c.at[step - 1])
            copy.start()
            copy.wait()
        for s in range(per):
            take_relay(0, s)
            take_far_e(s)
        for s in range(per - 1):
            start_cross_s(s)
        for s in range(per):
            take_end(0, s)
        host(0)
        local[2].wait()
        acc[...] = jnp.zeros_like(acc)
        each_full(0, q, 1, shrink)
        each_part(0, near_outer, 1, shrink)
        for s in range(per):
            if s == per - 1:
                start_cross_s(s)
            take_relay(1, s)
        for s in range(per - 1):
            take_s(s)
            take_end(1, s)
        each_part(0, far_outer, 1, shrink)
        take_s(per - 1)
        shared_s()
        far_own()
        host(1)

        @pl.loop(0, w)
        def _(k):
            back((u + k) % w).start()

        take_end(1, per - 1)
        each_full(0, far_inner, 1, shrink)
        shr[...] = acc[...].astype(shr.dtype)
        each_full(1, q, 1, expand)
        each_part(1, far_inner, 1, expand)
        each_part(1, near_outer, 1, expand)
        each_part(1, far_outer, 1, expand)

        for step in range(1, groups):
            ids_copy(step).wait_send()
        for s in range(per):
            across(1, s).wait_send()
            for chosen, copy in cross_s(0, s):
                @pl.when(chosen)
                def _(copy=copy):
                    copy.wait_send()
            part_done(1, s, far_inner, far_out.at[0, s], fo_s.at[0, s], both)
            for p in range(2):
                forward(p, s).wait_send()
                part_done(p, s, far_outer, far_out.at[1 + p, s], fo_s.at[1 + p, s], both)
                part_done(p, s, near_outer, rel_out.at[p, s], ro_s.at[p, s], near)
        for i in range(units):
            @pl.when(i // per == g)
            def _(i=i):
                for step in range(1, groups):
                    share_s(i, step).wait_send()

        @pl.loop(1, w)
        def _(k):
            far_copy((u + k) % w).wait_send()

        @pl.loop(0, w)
        def _(k):
            near_copy(1, near_outer, (u + k) % w).wait_send()
            back((u + k) % w).wait_send()

    @pl.when(outer)
    def _():
        for s in range(per):
            relay(0, s).start()
        pass_rows(0).start()
        for i in range(side):
            visit(0, i).start()
        local[0].wait()
        near_own(0)
        pass_rows(1).start()
        local[1].wait()
        near_own(1)

        def rows_got(f):
            remote(tokrel.at[f], tokrel.at[f], ty_s.at[f], ty_r.at[f], g, me).wait_recv()

        rows_got(0)
        for i in range(side):
            visit_mate(0, i).start()
        for s in range(per):
            relay(1, s).start()
        for i in range(side):
            visit(1, i).start()
        rows_got(1)
        for i in range(side):
            visit_mate(1, i).start()
        local[2].wait()
        acc[...] = jnp.zeros_like(acc)
        each_full(0, q, 1, shrink)
        each_part(0, far_outer, 0, shrink)

        @pl.loop(0, w)
        def _(k):
            v = (u - k + w) % w
            came_back(v).wait_recv()
            for b in range(blocks):
                at = (b % 2) * rank
                acc[b] += pgot[v, b // 2, :, at:at + rank]

        shr[...] = acc[...].astype(shr.dtype)
        each_full(1, q, 1, expand)
        each_full(1, near_inner, 0, expand)
        each_part(1, far_inner, 0, expand)
        each_part(1, far_outer, 0, expand)

        for f in range(2):
            pass_rows(f).wait_send()
            for i in range(side):
                visit(f, i).wait_send()
                visit_mate(f, i).wait_send()
        for p in range(2):
            for s in range(per):
                relay(p, s).wait_send()

    for p in range(2):
        @pl.loop(1, w)
        def _(k, p=p):
            near_copy(p, q, (u + k) % w).wait_send()


def body(n, groups, tokens, shrink_panels, expand_panels, adapter_scale, block_adapter, shard_counts):
    rows, width = tokens.shape
    adapters, feats, rank = shrink_panels.shape
    blocks = rows // BLOCK
    h, w = n // 2, n // 4
    units = rank // UNIT
    per = units // groups
    side = w // 2
    bf16 = tokens.dtype
    dma = pltpu.SemaphoreType.DMA
    smem = pl.BlockSpec(memory_space=pltpu.SMEM)
    hbm = pl.BlockSpec(memory_space=pl.ANY)
    panel = pltpu.VMEM((adapters, rank, feats), bf16)
    moved = (units, blocks, UNIT, feats)
    one = (blocks, UNIT, feats)
    slot = pltpu.VMEM((n, *moved), bf16)
    sums = pltpu.VMEM((w, (blocks + 1) // 2, BLOCK, 2 * rank), jnp.float32)
    ids = jnp.swapaxes(block_adapter, 0, 1)
    return pl.pallas_call(
        functools.partial(kernel, n, groups),
        out_shape=pltpu.VMEM((rows, width), bf16),
        in_specs=[smem, smem, smem, hbm, hbm, hbm, hbm],
        out_specs=pl.BlockSpec(memory_space=pltpu.VMEM),
        scratch_shapes=[
            pltpu.VMEM((rows, width), bf16),
            panel, panel,
            pltpu.VMEM((w, *moved), bf16),
            pltpu.VMEM((2 * w, *moved), bf16),
            pltpu.VMEM((w, *moved), bf16),
            pltpu.VMEM((3, per, groups, h, *one), bf16),
            pltpu.VMEM((2, per, groups, w, *one), bf16),
            slot, slot,
            pltpu.VMEM((2, w, rows, feats), bf16),
            pltpu.VMEM((2, rows, side * feats), bf16),
            sums, sums,
            pltpu.VMEM((blocks, BLOCK, rank), jnp.float32),
            pltpu.VMEM((blocks, BLOCK, rank), bf16),
            pltpu.VMEM((groups, 1, n * blocks), jnp.int32),
            pltpu.SMEM((groups, 1, n * blocks), jnp.int32),
            dma((4,)), dma((groups,)), dma((groups,)), dma((groups,)),
            dma((w,)), dma((2 * w,)), dma((w,)),
            dma((3, per, groups, h)), dma((2, per, groups, w)), dma((2, n, units)),
            dma((2, per)), dma((2, per)), dma((2, per)), dma((2, units)),
            dma((2, per)), dma((2, per)), dma((units, groups)), dma((units,)),
            dma((2,)), dma((2,)), dma((2, 2, side)), dma((2, w)), dma((w,)), dma((w,)),
            *[pltpu.VMEM((adapters, UNIT, feats), bf16)] * (units + 5 * per),
        ],
        compiler_params=pltpu.CompilerParams(
            collective_id=0, has_side_effects=True, vmem_limit_bytes=56 * 1024 * 1024
        ),
    )(
        block_adapter[:, 0], adapter_scale, shard_counts, ids,
        tokens, jnp.swapaxes(shrink_panels, 1, 2), expand_panels,
    )


def solution(mesh):
    return jax.shard_map(
        functools.partial(body, mesh.shape["blk"], mesh.shape["groups"]),
        mesh=mesh,
        in_specs=(
            P(("groups", "blk"), None),
            P(None, "blk", None),
            P(None, None, "blk"),
            P(),
            P("groups", None),
            P("groups"),
        ),
        out_specs=P(("groups", "blk"), None),
        check_vma=False,
    )
```

time: 130 us -> 135 us (1.038)
  Pallas kernels: 127 us -> 133 us
    pallas_call x1, Pallas kernels: 127 us -> 133 us  [body(): pl.pallas_call(functools.partial(kernel, n, groups), out_shape=pltpu.VMEM...]
where the time goes in v2:
time: 135 us
  Pallas kernels  133 us (99%)
  local copies, waits for them, and re-layouts  2.02 us (1%)
    pallas_call x1, Pallas kernels, body(): pl.pallas_call(functools.partial(kernel, n, groups), out_shape=pltpu.VMEM...  133 us

profile of v2, /device:TPU:0, one launch (start us, length us, event | category | flops | bytes accessed | tf_op | source)
XLA Modules:
  0.0 134.8 jit_solution(11264946935497718974)
XLA Ops:
  0.0 132.8 %shard_map.64 = bf16[256,8192]{1,0:T(8,128)(2,1)S(1)} custom-call(s32[64]{0:T(128)} %bitcast.4, f32[32]{0:T(128)} %scale.1, s32[16]{0:T(128)} %counts.1, s32[1,64]{1,0:T(1,128)} %bitcast.5, bf16[256,8192]{1,0:T(8,128)(2,1)} %tok_h.1, bf16[32,64,512]{2,1,0:T(8,128)(2,1)} %bitcast.3, bf16[32,64,512]{2,1,0:T(8,128)(2,1)} %e_h.1), custom_call_target="tpu_custom_call" | custom-call | tf_op jit(solution)/shard_map/pallas_call | solution.py:526
  132.8 2.0 %copy.8 = bf16[256,8192]{1,0:T(8,128)(2,1)} copy(bf16[256,8192]{1,0:T(8,128)(2,1)S(1)} %shard_map.64) | data formatting | bytes 8388608
